TPU v7x, 256 devices: a whole 4x4x8 slice. The times are simulated.
256 devices in a mesh: occ: 16 (over z_hi, y, core), vir: 16 (over z_lo, x).
Axes of the slice: x: 4, y: 4, z: 8 (z_hi: 2, z_lo: 4; z = z_hi * 4 + z_lo), core: 2. Of those that a mesh axis runs over, the one named last changes fastest.
Arguments:
- amplitudes: bfloat16 [8192, 8192], P('occ', 'vir'), may hold values from -6 to 6
- hole_integrals: bfloat16 [8192, 8192], P('occ'), may hold values from -0.1875 to 0.1875
- particle_integrals: bfloat16 [8192, 8192], P('vir'), may hold values from -0.25 to 0.25
- occ_irrep: int32 [128], replicated, may hold values from 0 to 7
- vir_irrep: int32 [128], replicated, may hold values from 0 to 7
- occ_energy: float32 [8192], P('occ'), may hold values from -1.5 to -0.5
- vir_energy: float32 [8192], P('vir'), may hold values from 0.5 to 2.5
Outputs:
- update: float32 [8192, 8192], P('vir', 'occ')
All inputs are finite; a program needn't handle non-finite values.
Results may differ from a plain program's by a relative error of at most 0.0003.
Values may be sent and summed in bfloat16 or wider, within the bound.
No kernel may reach another device: no remote copies, remote signals or barrier semaphores. Data moves between devices by JAX's collectives and lax.ppermute only.
A program may use at most 128 MiB of HBM per device.

v0:
```python
import jax
import jax.numpy as jnp
from jax import lax
from jax.sharding import PartitionSpec as P

TILE = 64


def per_device(
    amplitudes, hole_integrals, particle_integrals, occ_irrep, vir_irrep, occ_energy, vir_energy
):
    own_rows = amplitudes.shape[0]
    own_pairs = amplitudes.shape[1]
    zero_value = jnp.zeros((), jnp.bfloat16)
    occ_labels = jnp.repeat(occ_irrep, TILE)
    vir_labels = jnp.repeat(vir_irrep, TILE)
    own_occ = lax.dynamic_slice_in_dim(occ_labels, lax.axis_index("occ") * own_rows, own_rows)
    own_vir = lax.dynamic_slice_in_dim(vir_labels, lax.axis_index("vir") * own_pairs, own_pairs)
    hole_masked = jnp.where(own_occ[:, None] == occ_labels[None, :], hole_integrals, zero_value)
    contract_first = (((0,), (1,)), ((), ()))
    hole = lax.dot_general(
        lax.all_gather(amplitudes, "occ", axis=0, tiled=True),
        hole_masked,
        contract_first,
        preferred_element_type=jnp.float32,
    )
    slab_masked = jnp.where(own_vir[:, None] == vir_labels[None, :], particle_integrals, zero_value)
    particle = lax.psum_scatter(
        lax.dot_general(
            slab_masked, amplitudes, contract_first, preferred_element_type=jnp.float32
        ),
        "vir",
        scatter_dimension=0,
        tiled=True,
    )
    energy_gap = vir_energy[:, None] - occ_energy[None, :]
    return (hole + particle) / energy_gap


def solution(mesh):
    placed = (P("occ", "vir"), P("occ", None), P("vir", None), P(), P(), P("occ"), P("vir"))
    return jax.shard_map(
        per_device, mesh=mesh, in_specs=placed, out_specs=P("vir", "occ"), check_vma=False
    )
```

profile of v0, /device:TPU:65, one launch (start us, length us, event | category | flops | bytes accessed | tf_op | source)
XLA Modules:
  0.0 290.1 jit_solution(7640333086408449033)
XLA Ops:
  7.4 0.0 all-gather.2.cloned.1.call-start
  7.4 0.7 all-gather.2.cloned.1.call-update
  8.1 0.0 reduce-scatter.2.cloned.1.call-start
  8.1 0.7 broadcast_in_dim.17
  8.9 0.1 reshape.13
  9.0 0.1 dynamic_slice.7
  9.0 14.0 %fusion.1 = f32[8192,512]{0,1:T(8,128)} fusion(bf16[512,512]{1,0:T(8,128)(2,1)} %param.7, bf16[512,8192]{1,0:T(8,128)(2,1)} %param.9, s32[8192]{0:T(1024)S(1)} %reshape.13, s32[512]{0:T(512)S(1)} %dynamic_slice.7), kind=kOutput, calls=%fused_computation.3 | convolution fusion | flops 4303355904 | bytes 25724928 | tf_op jit(solution)/shard_map/dot_general | solution.py:29
  23.0 0.0 copy-start
  23.0 0.0 copy-start.1
  23.0 0.0 copy-start.2
  23.0 0.0 reduce-scatter.2.cloned.1.call-update
  23.0 0.6 copy-done
  23.7 0.1 broadcast_in_dim.15
  23.7 0.1 reshape.12
  23.8 0.1 dynamic_slice.6
  23.9 246.9 %all-gather.2.cloned.1.call-done = bf16[8192,512]{1,0:T(8,128)(2,1)} async-done(((bf16[512,512]{1,0:T(8,128)(2,1)}), bf16[8192,512]{1,0:T(8,128)(2,1)}) %all-gather.2.cloned.1.call-update) | async-done | bytes 8388624 | tf_op jit(solution)/shard_map/all_gather | solution.py:22
  270.8 0.0 reduce-scatter.2.cloned.1.call-done
  270.8 0.0 copy-done.1
  270.8 0.0 copy-done.2
  270.8 10.5 %subtract_divide_fusion = f32[512,512]{0,1:T(8,128)S(1)} fusion(f32[512,512]{0,1:T(8,128)} %reduce-scatter.2.cloned.1.call-done, bf16[8192,512]{1,0:T(8,128)(2,1)} %all-gather.2.cloned.1.call-done, bf16[512,8192]{1,0:T(8,128)(2,1)} %param.8, s32[8192]{0:T(1024)S(1)} %reshape.12, s32[512]{0:T(512)S(1)} %dynamic_slice.6, f32[512]{0:T(512)S(1)} %copy-done.1, ...), kind=kOutput, calls=%fused_computation.12 | convolution fusion | flops 4304142336 | bytes 18913280 | tf_op jit(solution)/shard_map/dot_general | solution.py:21
  281.3 1.3 copy.11
Async XLA Ops:
  7.4 263.4 %all-gather.2.cloned.1.call-start = ((), (), s32[]{:S(2)}) async-start(), calls=%async_computation.1 | async-start | bytes 8912896 | tf_op jit(solution)/shard_map/all_gather | solution.py:22
  8.1 262.7 %reduce-scatter.2.cloned.1.call-start = ((), (), s32[]{:S(2)}) async-start(), calls=%async_computation.2 | async-start | bytes 17825792 | tf_op jit(solution)/shard_map/reduce_scatter | solution.py:28
  23.0 0.7 copy-start
  23.0 247.8 %copy-start.1 = (f32[512]{0:T(512)S(1)}, f32[512]{0:T(512)}, u32[]{:S(2)}) copy-start(f32[512]{0:T(512)} %param.12) | copy-start | bytes 6148
  23.0 247.8 %copy-start.2 = (f32[512]{0:T(512)S(1)}, f32[512]{0:T(512)}, u32[]{:S(2)}) copy-start(f32[512]{0:T(512)} %param.13) | copy-start | bytes 6148
Sparse Core Ops, SparseCore 0:
  10.9 259.8 all-gather.1
Sparse Core Ops, SparseCore 1:
  23.1 234.3 reduce-scatter.1
where the time goes:
time: 290 us
  waiting for transfers between devices  248 us (86%)
  matrix products  24.5 us (8%)
  between operations  14.9 us (5%)
  local copies, waits for them, and re-layouts  3.04 us (1%)
    all_gather x1, waiting for transfers between devices, per_device(): lax.all_gather(amplitudes, 'occ', axis=0, tiled=True)  247 us
    dot_general x1, matrix products, per_device(): lax.dot_general(slab_masked, amplitudes, contract_first, preferred_elemen...  14 us
    dot_general x1, matrix products, per_device(): lax.dot_general(lax.all_gather(amplitudes, 'occ', axis=0, tiled=True), ho...  10.5 us
  transfers between devices with their start and end apart: 2, of which 1 were waited for; matrix products, arithmetic and copies ran while one was open for 5% of the time, Pallas kernels for 0%

commit v1 on v0

--- a/solution.py
+++ b/solution.py
@@ -19,7 +19,9 @@
     hole_masked = jnp.where(own_occ[:, None] == occ_labels[None, :], hole_integrals, zero_value)
     contract_first = (((0,), (1,)), ((), ()))
     hole = lax.dot_general(
-        lax.all_gather(amplitudes, "occ", axis=0, tiled=True),
+        jnp.concatenate(
+            lax.all_to_all(jnp.stack([amplitudes] * lax.axis_size("occ")), "occ", 0, 0), axis=0
+        ),
         hole_masked,
         contract_first,
         preferred_element_type=jnp.float32,

time: 290 us -> 441 us (1.52)
  the two profiles are of different devices: /device:TPU:65 before, /device:TPU:8 now
where the time goes in v1:
time: 441 us
  waiting for transfers between devices  384 us (87%)
  matrix products  24.5 us (6%)
  between operations  13.4 us (3%)
  starting transfers between devices  11.7 us (3%)
  local copies, waits for them, and re-layouts  7.48 us (2%)
    reduce_scatter x1, waiting for transfers between devices, per_device(): lax.psum_scatter(lax.dot_general(slab_masked, amplitudes, contract_first,...  202 us
    all_to_all x1, waiting for transfers between devices, per_device(): lax.all_to_all(jnp.stack([amplitudes] * lax.axis_size('occ')), 'occ', 0, 0)  182 us
    dot_general x1, matrix products, per_device(): lax.dot_general(slab_masked, amplitudes, contract_first, preferred_elemen...  14 us
    all_to_all x1, starting transfers between devices, per_device(): lax.all_to_all(jnp.stack([amplitudes] * lax.axis_size('occ')), 'occ', 0, 0)  11.7 us
    dot_general x1, matrix products, per_device(): lax.dot_general(jnp.concatenate(lax.all_to_all(jnp.stack([amplitudes] * l...  10.5 us
  transfers between devices with their start and end apart: 2, of which 2 were waited for; matrix products, arithmetic and copies ran while one was open for 1% of the time, Pallas kernels for 0%

profile of v1, /device:TPU:8, one launch (start us, length us, event | category | flops | bytes accessed | tf_op | source)
XLA Modules:
  0.0 441.0 jit_solution(1911743885842531731)
XLA Ops:
  6.5 0.0 reduce-scatter.2.cloned.1.call-start
  6.5 0.7 broadcast_in_dim.17
  7.3 0.1 reshape.19
  7.3 0.1 dynamic_slice.7
  7.4 14.0 %fusion.1 = f32[8192,512]{0,1:T(8,128)} fusion(bf16[512,512]{1,0:T(8,128)(2,1)} %param.7, bf16[512,8192]{1,0:T(8,128)(2,1)} %param.9, s32[8192]{0:T(1024)S(1)} %reshape.19, s32[512]{0:T(512)S(1)} %dynamic_slice.7), kind=kOutput, calls=%fused_computation.3 | convolution fusion | flops 4303355904 | bytes 25724928 | tf_op jit(solution)/shard_map/dot_general | solution.py:31
  21.4 0.0 copy-start
  21.4 0.0 reduce-scatter.2.cloned.1.call-update
  21.4 1.0 copy-done
  22.4 4.0 stack.2
  26.5 0.0 copy-start.1
  26.5 0.0 copy-start.2
  26.5 0.0 copy-start.3
  26.5 11.7 %all-to-all-start = ((bf16[16,512,512]{2,1,0:T(8,128)(2,1)}), bf16[16,512,512]{2,1,0:T(8,128)(2,1)}, u32[]{:S(2)}, u32[]{:S(2)}) async-start(bf16[16,512,512]{2,1,0:T(8,128)(2,1)} %stack.2), calls=%async_computation | async-start | bytes 16777216 | tf_op jit(solution)/shard_map/all_to_all | solution.py:23
  38.2 0.0 copy-done.1
  38.2 0.1 broadcast_in_dim.15
  38.3 0.1 reshape.17
  38.3 0.1 dynamic_slice.6
  38.4 182.4 %all-to-all-done = bf16[16,512,512]{2,1,0:T(8,128)(2,1)} async-done(((bf16[16,512,512]{2,1,0:T(8,128)(2,1)}), bf16[16,512,512]{2,1,0:T(8,128)(2,1)}, u32[]{:S(2)}, u32[]{:S(2)}) %all-to-all-start) | async-done | bytes 8388640 | tf_op jit(solution)/shard_map/all_to_all | solution.py:23
  220.8 201.5 %reduce-scatter.2.cloned.1.call-done = f32[512,512]{0,1:T(8,128)} async-done(((f32[8192,512]{0,1:T(8,128)}), f32[512,512]{0,1:T(8,128)}) %reduce-scatter.2.cloned.1.call-update) | async-done | bytes 1048592 | tf_op jit(solution)/shard_map/reduce_scatter | solution.py:30
  422.3 0.0 copy-done.2
  422.3 0.0 copy-done.3
  422.3 10.5 %subtract_divide_fusion = f32[512,512]{0,1:T(8,128)S(1)} fusion(f32[512,512]{0,1:T(8,128)} %reduce-scatter.2.cloned.1.call-done, bf16[8192,512]{1,0:T(8,128)(2,1)} %bitcast, bf16[512,8192]{1,0:T(8,128)(2,1)} %param.8, s32[8192]{0:T(1024)S(1)} %reshape.17, s32[512]{0:T(512)S(1)} %dynamic_slice.6, f32[512]{0:T(512)S(1)} %copy-done.2, f32[512]{0:T(512)S(1)} %copy-done.3), kind=kOutput, calls=%fused_computation.12 | convolution fusion | flops 4304142336 | bytes 18913280 | tf_op jit(solution)/shard_map/dot_general | solution.py:21
  432.9 1.3 copy.11
Async XLA Ops:
  6.5 415.8 %reduce-scatter.2.cloned.1.call-start = ((), (), s32[]{:S(2)}) async-start(), calls=%async_computation.2 | async-start | bytes 17825792 | tf_op jit(solution)/shard_map/reduce_scatter | solution.py:30
  21.4 1.0 copy-start
  26.5 11.7 %copy-start.1 = (s32[128]{0:T(128)S(1)}, s32[128]{0:T(128)}, u32[]{:S(2)}) copy-start(s32[128]{0:T(128)} %param.10) | copy-start | bytes 1540
  26.5 395.8 %copy-start.2 = (f32[512]{0:T(512)S(1)}, f32[512]{0:T(512)}, u32[]{:S(2)}) copy-start(f32[512]{0:T(512)} %param.12) | copy-start | bytes 6148
  26.5 395.8 %copy-start.3 = (f32[512]{0:T(512)S(1)}, f32[512]{0:T(512)}, u32[]{:S(2)}) copy-start(f32[512]{0:T(512)} %param.13) | copy-start | bytes 6148
  26.5 194.3 %all-to-all-start = ((bf16[16,512,512]{2,1,0:T(8,128)(2,1)}), bf16[16,512,512]{2,1,0:T(8,128)(2,1)}, u32[]{:S(2)}, u32[]{:S(2)}) async-start(bf16[16,512,512]{2,1,0:T(8,128)(2,1)} %stack.2), calls=%async_computation | async-start | bytes 16777216 | tf_op jit(solution)/shard_map/all_to_all | solution.py:23
Sparse Core Ops, SparseCore 0:
  21.5 400.7 reduce-scatter.1
